TPU v7x, 32 devices: a whole 2x2x4 slice. The times are simulated.
32 devices in a mesh: grp: 4 (over y, x), ep: 8 (over z, core).
Axes of the slice: x: 2, y: 2, z: 4, core: 2. Of those that a mesh axis runs over, the one named last changes fastest.
Arguments:
- layer_in: bfloat16 [4096, 1536], P(('grp', 'ep')), may hold values from -6 to 6
- segments: int32 [4096], P(('grp', 'ep')), may hold values from 0 to 4, as said below
- routes: int32 [4096, 8], P(('grp', 'ep')), may hold values from 0 to 23, all different within a row; in each aligned block of 128 rows (0 to 127, 128 to 255, ...) at most 56 rows name the same one
- qkv_weight: bfloat16 [2560, 1536], P('ep'), may hold values from -0.15625 to 0.15625
- out_weight: bfloat16 [1536, 1536], P('ep'), may hold values from -1.25 to 1.25
- router_weight: bfloat16 [24, 1536], P('ep'), may hold values from -0.078125 to 0.078125
- norm1_gain: bfloat16 [1536], P('ep'), may hold values from 0.25 to 1.75
- norm2_gain: bfloat16 [1536], P('ep'), may hold values from 0.25 to 1.75
- w_gate: bfloat16 [24, 512, 1536], P('ep'), may hold values from -0.15625 to 0.15625
- w_up: bfloat16 [24, 512, 1536], P('ep'), may hold values from -0.15625 to 0.15625
- w_down: bfloat16 [24, 512, 1536], P('ep'), may hold values from -1 to 1
- out_cotangent: bfloat16 [4096, 1536], P(('grp', 'ep')), may hold values from -6 to 6
Outputs:
- layer_out: bfloat16 [4096, 1536], P(('grp', 'ep'))
- grad_in: bfloat16 [4096, 1536], P(('grp', 'ep'))
- grad_qkv: float32 [2560, 1536], P('ep')
- grad_out_weight: float32 [1536, 1536], P('ep')
- grad_router: float32 [24, 1536], P('ep')
- grad_norm1: float32 [1536], P('ep')
- grad_norm2: float32 [1536], P('ep')
- grad_gate: float32 [24, 512, 1536], P('ep', None, 'grp')
- grad_up: float32 [24, 512, 1536], P('ep', None, 'grp')
- grad_down: float32 [24, 512, 1536], P('ep', None, 'grp')
Inputs may be any that keep to these rules, and one draw needn't show every extreme that they name: `segments`: within each sequence of 1024 tokens the numbers start at 0 and rise by one at each new document. Every document has at most 800 tokens and each sequence holds one of exactly 800; every document but a sequence's last has 60 or more. `routes`: each row names 8 different experts. In the rows of one device (128 aligned rows) no expert is named by more than 56 rows, a bound that some block reaches.
All inputs are finite; a program needn't handle non-finite values.
Results may differ from a plain program's by a relative error of at most 0.025.
Values may be sent and summed in bfloat16 or wider, within the bound.
No kernel may reach another device: no remote copies, remote signals or barrier semaphores. Data moves between devices by JAX's collectives and lax.ppermute only.
A program may use at most 192 MiB of HBM per device.

v0:
```python
import jax
import jax.numpy as jnp
from jax import lax
from jax.sharding import PartitionSpec as P

QUERY_HEADS = 24
KEY_VALUE_HEADS = 8
HEAD_DIMENSION = 64
TOPK = 8
eps = 1e-06
theta = 10000.0
negative_large = -1e30
f32 = jnp.float32
bf16 = jnp.bfloat16


def angles(token_positions, head_size):
    half = head_size // 2
    freq = theta ** (-jnp.arange(half, dtype=f32) * 2.0 / head_size)
    angle = token_positions.astype(f32)[:, None] * freq[None, :]
    return (jnp.cos(angle)[:, None, :], jnp.sin(angle)[:, None, :])


def rotate(value_matrix, cosine_table, sine_table):
    half = value_matrix.shape[-1] // 2
    first = value_matrix[..., :half]
    second = value_matrix[..., half:]
    return jnp.concatenate(
        [first * cosine_table - second * sine_table, second * cosine_table + first * sine_table],
        axis=-1,
    )


def norm_back(delta, normed, scale, gain):
    scaled = delta * gain
    return scale * (scaled - normed * jnp.mean(scaled * normed, axis=-1, keepdims=True))


def head_plan(devices):
    per_query = QUERY_HEADS // devices
    per_key = KEY_VALUE_HEADS // devices
    blocks = QUERY_HEADS + 2 * KEY_VALUE_HEADS
    own = blocks // devices

    def place(block):
        if block < QUERY_HEADS:
            return (block // per_query, block % per_query)
        block -= QUERY_HEADS
        if block < KEY_VALUE_HEADS:
            return (block // per_key, per_query + block % per_key)
        block -= KEY_VALUE_HEADS
        return (block // per_key, per_query + per_key + block % per_key)

    left = [[(s, *place(i * own + s)) for s in range(own)] for i in range(devices)]
    rounds = []
    for _ in range(own):
        taken = {}

        def assign(i, seen):
            for edge in left[i]:
                j = edge[1]
                if j in seen:
                    continue
                seen.add(j)
                if j not in taken or assign(taken[j][0], seen):
                    taken[j] = (i, edge)
                    return True
            return False

        for i in range(devices):
            assign(i, set())
        source_slot, target, target_slot = ([0] * devices, [0] * devices, [0] * devices)
        for j, (i, edge) in taken.items():
            source_slot[i], target[i], target_slot[j] = (edge[0], j, edge[2])
            left[i].remove(edge)
        rounds.append((source_slot, target, target_slot))
    return rounds


def move_blocks(blocks, pick, pairs, order):
    got = [
        lax.ppermute(lax.dynamic_index_in_dim(blocks, slot, 0, keepdims=False), "ep", pair)
        for slot, pair in zip(pick, pairs)
    ]
    return jnp.stack(got)[order]


def local(
    layer_in,
    segments,
    routes,
    qkv_weight,
    out_weight,
    router_weight,
    norm1_gain,
    norm2_gain,
    w_gate,
    w_up,
    w_down,
    out_cotangent,
):
    tokens, width = layer_in.shape
    devices = lax.axis_size("ep")
    me = lax.axis_index("ep")
    copies = lax.axis_size("grp")
    mine = w_gate.shape[0]
    hidden = w_gate.shape[1]
    experts = mine * devices
    seq = tokens * devices
    capacity = 9 * tokens * TOPK // (8 * mine)
    heads = QUERY_HEADS // devices
    keys = KEY_VALUE_HEADS // devices
    group = heads // keys
    hd = HEAD_DIMENSION
    scale = hd ** (-0.5)
    x_all = lax.all_gather(layer_in, "ep", axis=0, tiled=True)
    gain_width = norm1_gain.shape[0]
    small = jnp.concatenate(
        [
            router_weight.reshape(-1),
            norm1_gain,
            norm2_gain,
            routes.T.astype(bf16).reshape(-1),
            segments.astype(bf16),
        ]
    )
    small_all = lax.all_gather(small, "ep", axis=0, tiled=False)
    cut = mine * width
    full_router = small_all[:, :cut].reshape(experts, width)
    gain_one = small_all[:, cut : cut + gain_width].reshape(1, width).astype(f32)
    gain_two = small_all[:, cut + gain_width : cut + 2 * gain_width].reshape(1, width).astype(f32)
    cut += 2 * gain_width
    routes_all = small_all[:, cut : cut + tokens * TOPK].reshape(devices, TOPK, tokens)
    routes_all = routes_all.transpose(1, 0, 2).reshape(TOPK, seq).astype(jnp.int32)
    seg_all = small_all[:, cut + tokens * TOPK :].reshape(seq)
    rounds = head_plan(devices)
    slots = len(rounds)
    to_heads = [[(i, t[i]) for i in range(devices)] for _, t, _ in rounds]
    to_rows = [[(b, a) for a, b in pair] for pair in to_heads]
    pick_row = [jnp.array(s, jnp.int32)[me] for s, _, _ in rounds]
    pick_head = [jnp.array(s, jnp.int32)[me] for _, _, s in rounds]
    order_head = jnp.array(
        [[[r[2][d] for r in rounds].index(s) for s in range(slots)] for d in range(devices)],
        jnp.int32,
    )[me]
    order_row = jnp.array(
        [[[r[0][d] for r in rounds].index(s) for s in range(slots)] for d in range(devices)],
        jnp.int32,
    )[me]
    block_rows = qkv_weight.shape[0] // slots
    qkv_heads = move_blocks(
        qkv_weight.reshape(slots, block_rows, width), pick_row, to_heads, order_head
    ).reshape(slots * block_rows, width)
    full_out = lax.all_gather(out_weight, "ep", axis=0, tiled=True)
    expert_row = jnp.arange(experts, dtype=jnp.int32)[:, None, None]
    chosen = jnp.any(routes_all[None] == expert_row, axis=1)
    own_chosen = lax.dynamic_slice_in_dim(chosen, me * mine, mine, 0)
    before = (
        jnp.arange(seq, dtype=jnp.int32)[:, None] < jnp.arange(seq, dtype=jnp.int32)[None, :]
    ).astype(bf16)
    rank = jnp.einsum(
        "es,st->et", own_chosen.astype(bf16), before, preferred_element_type=f32
    ).astype(jnp.int32)
    rank = jnp.where(own_chosen, rank, -1)
    places = jnp.arange(capacity, dtype=jnp.int32)[None, :, None]
    pick = rank[:, None, :] == places
    pick_low = pick.astype(bf16).reshape(mine * capacity, seq)
    residual_all = x_all.astype(f32)
    scale_one_all = lax.rsqrt(jnp.mean(residual_all * residual_all, axis=-1, keepdims=True) + eps)
    normed_all = residual_all * scale_one_all
    x_low = (normed_all * gain_one).astype(bf16)
    projected = jnp.einsum("td,cd->tc", x_low, qkv_heads, preferred_element_type=f32)
    positions = jnp.arange(seq, dtype=jnp.int32)
    cosine_table, sine_table = angles(positions, hd)
    turned = rotate(
        projected[:, : (heads + keys) * hd].reshape(seq, heads + keys, hd), cosine_table, sine_table
    ).astype(bf16)
    query = turned[:, :heads].reshape(seq, keys, group, hd).transpose(1, 2, 0, 3)
    key = turned[:, heads:].transpose(1, 0, 2)
    value = (
        projected[:, (heads + keys) * hd :].astype(bf16).reshape(seq, keys, hd).transpose(1, 0, 2)
    )
    valid = (seg_all[:, None] == seg_all[None, :]) & (positions[None, :] <= positions[:, None])
    score = jnp.einsum("hgqd,hkd->hgqk", query, key, preferred_element_type=f32) * scale
    score = jnp.where(valid, score, negative_large)
    top = jnp.max(score, axis=-1, keepdims=True)
    weight = jnp.where(valid, jnp.exp(score - top), 0.0)
    prob = weight / jnp.sum(weight, axis=-1, keepdims=True)
    prob_low = prob.astype(bf16)
    attended = jnp.einsum("hgqk,hkd->hgqd", prob_low, value, preferred_element_type=f32)
    mixed_heads = attended.transpose(2, 0, 1, 3).reshape(seq, heads * hd).astype(bf16)
    mixed = lax.all_to_all(mixed_heads, "ep", split_axis=0, concat_axis=1, tiled=True)
    branch = jnp.einsum("tc,dc->td", mixed, full_out, preferred_element_type=f32)
    hidden_one = layer_in.astype(f32) + branch
    scale_two = lax.rsqrt(jnp.mean(hidden_one * hidden_one, axis=-1, keepdims=True) + eps)
    normed_two = hidden_one * scale_two
    x_two = (normed_two * gain_two).astype(bf16)
    x_two_all = lax.all_gather(x_two, "ep", axis=0, tiled=True)
    late_cotangent, late_mixed, _ = lax.optimization_barrier((out_cotangent, mixed, x_two))
    g_all = lax.all_gather(late_cotangent, "ep", axis=0, tiled=True)
    mixed_all = lax.all_gather(late_mixed, "ep", axis=0, tiled=True)
    logits = jnp.einsum("ed,td->et", full_router, x_two_all, preferred_element_type=f32)
    logits = jnp.where(chosen, logits, negative_large)
    raised = jnp.where(chosen, jnp.exp(logits - jnp.max(logits, axis=0, keepdims=True)), 0.0)
    gates = raised / jnp.sum(raised, axis=0, keepdims=True)
    own_gates = lax.dynamic_slice_in_dim(gates, me * mine, mine, 0)
    place_gate = jnp.sum(jnp.where(pick, own_gates[:, None, :], 0.0), axis=-1)[:, :, None]

    def gather(rows):
        picked = jnp.einsum("pt,td->pd", pick_low, rows, preferred_element_type=f32)
        return picked.astype(bf16).reshape(mine, capacity, width)

    def scatter(rows):
        back = jnp.einsum(
            "pt,pd->td", pick_low, rows.reshape(mine * capacity, width), preferred_element_type=f32
        )
        return back.astype(bf16)

    def shares(left, right):
        grad = jnp.einsum("jcf,jcd->jfd", left, right, preferred_element_type=f32).astype(bf16)
        grad = grad.reshape(mine * hidden, copies, width // copies).transpose(1, 0, 2)
        return grad.reshape(copies * mine * hidden, width // copies)

    def grp_sum(part):
        total = lax.psum_scatter(part, "grp", scatter_dimension=0, tiled=True)
        return total.astype(f32).reshape(mine, hidden, width // copies)

    dense_in = gather(x_two_all)
    dense_g = gather(g_all)
    gate_pre = jnp.einsum("jcd,jfd->jcf", dense_in, w_gate, preferred_element_type=f32)
    up_pre = jnp.einsum("jcd,jfd->jcf", dense_in, w_up, preferred_element_type=f32)
    logistic = jax.nn.sigmoid(gate_pre)
    inner = (gate_pre * logistic * up_pre).astype(bf16)
    expert_out = jnp.einsum("jcf,jfd->jcd", inner, w_down, preferred_element_type=f32)
    place_dgate = jnp.sum(expert_out * dense_g.astype(f32), axis=-1)
    dgate_own = jnp.sum(jnp.where(pick, place_dgate[:, :, None], 0.0), axis=1)
    out_part = scatter((place_gate * expert_out).astype(bf16))
    dense_grad = (place_gate * dense_g.astype(f32)).astype(bf16)
    inner_grad = jnp.einsum("jcd,jfd->jcf", dense_grad, w_down, preferred_element_type=f32)
    gate_back = (inner_grad * up_pre * logistic * (1.0 + gate_pre * (1.0 - logistic))).astype(bf16)
    up_back = (inner_grad * gate_pre * logistic).astype(bf16)
    slot_grad = jnp.einsum(
        "jcf,jfd->jcd", gate_back, w_gate, preferred_element_type=f32
    ) + jnp.einsum("jcf,jfd->jcd", up_back, w_up, preferred_element_type=f32)
    back_part = scatter(slot_grad.astype(bf16))
    two_grad = lax.psum_scatter(back_part, "ep", scatter_dimension=0, tiled=True).astype(f32)
    dgate = lax.all_to_all(dgate_own, "ep", split_axis=1, concat_axis=0, tiled=True)
    down_part = shares(inner, dense_grad)
    gate_part = shares(gate_back, dense_in)
    up_part = shares(up_back, dense_in)
    delta = out_cotangent.astype(f32)
    gates_here = lax.dynamic_slice_in_dim(gates, me * tokens, tokens, 1)
    chosen_grad = gates_here * (dgate - jnp.sum(gates_here * dgate, axis=0, keepdims=True))
    logit_grad = chosen_grad.astype(bf16)
    router_grad = jnp.einsum("et,td->ed", logit_grad, x_two, preferred_element_type=f32)
    two_grad = two_grad + jnp.einsum(
        "et,ed->td", logit_grad, full_router, preferred_element_type=f32
    )
    gain_two_grad = jnp.sum(two_grad * normed_two, axis=0, keepdims=True)
    hidden_grad = delta + norm_back(two_grad, normed_two, scale_two, gain_two)
    hidden_low = hidden_grad.astype(bf16)
    mixing = jnp.einsum("td,dc->tc", hidden_low, full_out, preferred_element_type=f32)
    mixing_heads = lax.all_to_all(
        mixing.astype(bf16), "ep", split_axis=1, concat_axis=0, tiled=True
    )
    hidden_cols = lax.all_to_all(hidden_low, "ep", split_axis=1, concat_axis=0, tiled=True)
    change = mixing_heads.reshape(seq, keys, group, hd).transpose(1, 2, 0, 3)
    prob_grad = jnp.einsum("hgqd,hkd->hgqk", change, value, preferred_element_type=f32)
    row = jnp.sum(prob * prob_grad, axis=-1, keepdims=True)
    score_grad = (prob * (prob_grad - row)).astype(bf16)
    value_grad = jnp.einsum("hgqk,hgqd->hkd", prob_low, change, preferred_element_type=f32)
    query_grad = jnp.einsum("hgqk,hkd->hgqd", score_grad, key, preferred_element_type=f32) * scale
    key_grad = jnp.einsum("hgqk,hgqd->hkd", score_grad, query, preferred_element_type=f32) * scale
    turned_grad = jnp.concatenate(
        [query_grad.transpose(2, 0, 1, 3).reshape(seq, heads, hd), key_grad.transpose(1, 0, 2)],
        axis=1,
    )
    turned_grad = rotate(turned_grad, cosine_table, -sine_table).reshape(seq, (heads + keys) * hd)
    proj_grad = jnp.concatenate(
        [turned_grad, value_grad.transpose(1, 0, 2).reshape(seq, keys * hd)], axis=1
    ).astype(bf16)
    one_part = jnp.einsum("tc,cd->td", proj_grad, qkv_heads, preferred_element_type=f32)
    gain_one_grad = jnp.sum(one_part * normed_all, axis=0, keepdims=True)
    one_grad = lax.psum_scatter(
        one_part.astype(bf16), "ep", scatter_dimension=0, tiled=True
    ).astype(f32)
    qkv_grad = jnp.einsum("tc,td->cd", proj_grad, x_low, preferred_element_type=f32)
    out_grad = jnp.einsum("td,tc->dc", hidden_cols, mixed_all, preferred_element_type=f32)
    small_sum = lax.psum(
        jnp.concatenate([router_grad, gain_one_grad, gain_two_grad], axis=0), ("grp", "ep")
    )
    router_sum = lax.dynamic_slice_in_dim(small_sum[:experts], me * mine, mine, 0)
    gain_sums = lax.dynamic_slice_in_dim(small_sum[experts:], me * gain_width, gain_width, 1)
    qkv_sum = lax.psum(qkv_grad.astype(bf16), "grp")
    qkv_rows = move_blocks(
        qkv_sum.reshape(slots, block_rows, width), pick_head, to_rows, order_row
    ).reshape(slots * block_rows, width)
    out_sum = lax.psum(out_grad.astype(bf16), "grp")
    returned = lax.psum_scatter(out_part, "ep", scatter_dimension=0, tiled=True)
    layer_out = (hidden_one + returned.astype(f32)).astype(bf16)
    residual = layer_in.astype(f32)
    scale_one = lax.rsqrt(jnp.mean(residual * residual, axis=-1, keepdims=True) + eps)
    grad_in = (hidden_grad + norm_back(one_grad, residual * scale_one, scale_one, gain_one)).astype(
        bf16
    )
    return (
        layer_out,
        grad_in,
        qkv_rows.astype(f32),
        out_sum.astype(f32),
        router_sum,
        gain_sums[0],
        gain_sums[1],
        grp_sum(gate_part),
        grp_sum(up_part),
        grp_sum(down_part),
    )


def solution(mesh):
    in_specs = (
        P(("grp", "ep"), None),
        P(("grp", "ep")),
        P(("grp", "ep"), None),
        P("ep", None),
        P("ep", None),
        P("ep", None),
        P("ep"),
        P("ep"),
        P("ep", None, None),
        P("ep", None, None),
        P("ep", None, None),
        P(("grp", "ep"), None),
    )
    out_specs = (
        P(("grp", "ep"), None),
        P(("grp", "ep"), None),
        P("ep", None),
        P("ep", None),
        P("ep", None),
        P("ep"),
        P("ep"),
        P("ep", None, "grp"),
        P("ep", None, "grp"),
        P("ep", None, "grp"),
    )
    return jax.shard_map(local, mesh=mesh, in_specs=in_specs, out_specs=out_specs, check_vma=False)
```

profile of v0, /device:TPU:0, one launch (start us, length us, event | category | flops | bytes accessed | tf_op | source)
XLA Modules:
  0.0 818.6 jit_solution(11952017074831056703)
XLA Ops:
  27.4 5.0 collective-permute-start.2
  38.5 27.3 %all-gather = bf16[49152]{0:T(1024)(128)(2,1)S(1)} all-gather(bf16[6144]{0:T(1024)(128)(2,1)S(1)} %concatenate.21), channel_id=2, replica_groups=mesh['grp'=4,'ep'=8] {'ep'}, dimensions={0}, use_global_device_ids=true | all-gather | bytes 110592 | tf_op jit(solution)/shard_map/all_gather | solution.py:127
  76.0 3.2 fusion.45
  80.3 8.1 fusion.87
  88.5 6.1 fusion.29
  95.4 4.6 all-to-all-start
  100.2 20.0 %all-to-all-done = bf16[8,128,192]{1,2,0:T(8,128)(2,1)S(1)} async-done(((bf16[8,128,192]{1,2,0:T(8,128)(2,1)}), bf16[8,128,192]{1,2,0:T(8,128)(2,1)S(1)}, u32[]{:S(2)}, u32[]{:S(2)}) %all-to-all-start) | async-done | bytes 393248 | tf_op jit(solution)/shard_map/all_to_all | solution.py:192
  121.8 4.1 multiply_reduce_fusion.3
  131.0 33.4 %all-gather.11.cloned.1.call-done = bf16[1024,1536]{1,0:T(8,128)(2,1)} async-done(((bf16[128,1536]{1,0:T(8,128)(2,1)}), bf16[1024,1536]{1,0:T(8,128)(2,1)}) %all-gather.11.cloned.1.call-update) | async-done | bytes 3145744 | tf_op jit(solution)/shard_map/all_gather | solution.py:198
  168.7 6.2 convolution_convert_fusion.1
  178.4 3.9 multiply_convert_fusion.5
  182.3 20.8 %all-gather.13.cloned.1.call-done = bf16[1024,1536]{1,0:T(8,128)(2,1)} async-done(((bf16[128,1536]{1,0:T(8,128)(2,1)}), bf16[1024,1536]{1,0:T(8,128)(2,1)}) %all-gather.13.cloned.1.call-update) | async-done | bytes 3145744 | tf_op jit(solution)/shard_map/all_gather | solution.py:200
  203.1 6.2 convolution_convert_fusion
  209.3 9.0 %fusion.5 = (f32[3,384]{1,0:T(4,128)S(1)}, f32[3,384,1536]{2,1,0:T(8,128)}) fusion(bf16[3,384,1536]{2,1,0:T(8,128)(2,1)S(1)} %bitcast.239, bf16[3,384,512]{2,1,0:T(8,128)(2,1)S(1)} %copy-done.18, bf16[3,512,1536]{2,1,0:T(8,128)(2,1)} %param.34), kind=kOutput, calls=%fused_computation.17 | convolution fusion | flops 1817246592 | bytes 16519680 | tf_op jit(solution)/shard_map/jcf,jfd->jcd/dot_general | solution.py:234
  220.2 6.2 multiply_convert_fusion.3
  226.5 4.9 fusion.94
  231.4 10.6 %bitcast_convert_fusion = bf16[1024,1536]{1,0:T(8,128)(2,1)} fusion(s32[3,1024]{1,0:T(4,128)} %copy-done.30, f32[3,384,1536]{2,1,0:T(8,128)} %fusion.94, bf16[3,384,512]{2,1,0:T(8,128)(2,1)} %get-tuple-element.22, bf16[3,512,1536]{2,1,0:T(8,128)(2,1)} %param.33), kind=kOutput, calls=%fused_computation.23 | convolution fusion | flops 5442109440 | bytes 16134144 | tf_op jit(solution)/shard_map/pt,pd->td/dot_general | solution.py:214
  242.0 3.9 all-to-all-start.1
  246.0 5.7 all-to-all-done.1
  255.0 26.7 %reduce-scatter.9.cloned.1.call-done = bf16[128,1536]{1,0:T(8,128)(2,1)} async-done(((bf16[1024,1536]{1,0:T(8,128)(2,1)}), bf16[128,1536]{1,0:T(8,128)(2,1)}) %reduce-scatter.9.cloned.1.call-update) | async-done | bytes 393232 | tf_op jit(solution)/shard_map/reduce_scatter | solution.py:246
  287.2 3.9 convolution_convert_fusion.7
  293.0 4.1 all-to-all-start.2
  302.7 6.9 all-to-all-done.2
  309.6 4.1 all-to-all-start.3
  317.8 6.7 multiply_reduce_fusion
  324.6 8.2 %multiply_convert_fusion = bf16[3,1024,1024]{1,2,0:T(8,128)(2,1)S(1)} fusion(f32[3,1024,1024]{1,2,0:T(8,128)S(1)} %get-tuple-element.58, f32[3,1024]{1,0:T(4,128)S(1)} %get-tuple-element.57, f32[3,1024,1024]{1,2,0:T(8,128)} %get-tuple-element.47, f32[3,1024]{1,0:T(4,128)S(1)} %copy-done.36), kind=kLoop, calls=%fused_computation.3 | loop fusion | flops 12582912 | bytes 31481856 | tf_op jit(solution)/shard_map/convert_element_type | solution.py:270
  338.7 3.9 fusion.7
  343.5 4.4 convolution_convert_fusion.5
  347.9 4.0 convolution_convert_fusion.6
  352.2 7.2 convolution_convert_fusion.2
  359.4 9.1 %reshape.415 = bf16[1536,4,384]{2,1,0:T(4,128)(2,1)} reshape(bf16[3,512,1536]{2,1,0:T(8,128)(2,1)} %convolution_convert_fusion.2) | data formatting | bytes 9437184 | tf_op jit(solution)/shard_map/reshape | solution.py:221
  368.5 5.1 copy.92
  373.7 5.7 convolution_convert_fusion.3
  379.4 9.1 %reshape.411 = bf16[1536,4,384]{2,1,0:T(4,128)(2,1)} reshape(bf16[3,512,1536]{2,1,0:T(8,128)(2,1)} %convolution_convert_fusion.3) | data formatting | bytes 9437184 | tf_op jit(solution)/shard_map/reshape | solution.py:221
  388.4 5.1 copy.90
  393.6 5.7 convolution_convert_fusion.4
  399.3 9.1 %reshape.407 = bf16[1536,4,384]{2,1,0:T(4,128)(2,1)} reshape(bf16[3,512,1536]{2,1,0:T(8,128)(2,1)} %convolution_convert_fusion.4) | data formatting | bytes 9437184 | tf_op jit(solution)/shard_map/reshape | solution.py:221
  408.4 5.1 copy.88
  414.5 9.0 %bitcast_convert_fusion.1 = bf16[1024,1536]{1,0:T(8,128)(2,1)} fusion(f32[3,384,1536]{2,1,0:T(8,128)} %get-tuple-element.53, f32[3,384]{1,0:T(4,128)S(1)} %copy-done.40, s32[3,1024]{1,0:T(4,128)S(1)} %copy-done.32), kind=kOutput, calls=%fused_computation.24 | convolution fusion | flops 3630170112 | bytes 10240512 | tf_op jit(solution)/shard_map/pt,pd->td/dot_general | solution.py:214
  437.7 41.1 %all-reduce.4.cloned.1.call-done = f32[26,1536]{1,0:T(8,128)} async-done(((f32[26,1536]{1,0:T(8,128)}), f32[26,1536]{1,0:T(8,128)}) %all-reduce.4.cloned.1.call-update) | async-done | bytes 159760 | tf_op jit(solution)/shard_map/psum | solution.py:289
  481.2 63.6 %all-reduce.6.cloned.1.call-done = (bf16[5,64,1536]{2,1,0:T(8,128)(2,1)}, bf16[192,1536]{1,0:T(8,128)(2,1)}) async-done(((bf16[5,64,1536]{2,1,0:T(8,128)(2,1)}, bf16[192,1536]{1,0:T(8,128)(2,1)}), (bf16[5,64,1536]{2,1,0:T(8,128)(2,1)}, bf16[192,1536]{1,0:T(8,128)(2,1)})) %all-reduce.6.cloned.1.call-update) | async-done | bytes 1572880 | tf_op jit(solution)/shard_map/psum | solution.py:294
  547.5 6.1 collective-permute-start.9
  554.3 3.6 collective-permute-start.7
  564.8 40.0 %reduce-scatter.17.cloned.1.call-done = bf16[1536,384]{1,0:T(8,128)(2,1)} async-done(((bf16[6144,384]{1,0:T(8,128)(2,1)}), bf16[1536,384]{1,0:T(8,128)(2,1)}) %reduce-scatter.17.cloned.1.call-update) | async-done | bytes 1179664 | tf_op jit(solution)/shard_map/reduce_scatter | solution.py:225
  607.6 57.0 %reduce-scatter.15.cloned.1.call-done = bf16[1536,384]{1,0:T(8,128)(2,1)} async-done(((bf16[6144,384]{1,0:T(8,128)(2,1)}), bf16[1536,384]{1,0:T(8,128)(2,1)}) %reduce-scatter.15.cloned.1.call-update) | async-done | bytes 1179664 | tf_op jit(solution)/shard_map/reduce_scatter | solution.py:225
  667.6 57.0 %reduce-scatter.13.cloned.1.call-done = bf16[1536,384]{1,0:T(8,128)(2,1)} async-done(((bf16[6144,384]{1,0:T(8,128)(2,1)}), bf16[1536,384]{1,0:T(8,128)(2,1)}) %reduce-scatter.13.cloned.1.call-update) | async-done | bytes 1179664 | tf_op jit(solution)/shard_map/reduce_scatter | solution.py:225
  727.5 39.7 %reduce-scatter.11.cloned.1.call-done = bf16[128,1536]{1,0:T(8,128)(2,1)} async-done(((bf16[1024,1536]{1,0:T(8,128)(2,1)}), bf16[128,1536]{1,0:T(8,128)(2,1)}) %reduce-scatter.11.cloned.1.call-update) | async-done | bytes 393232 | tf_op jit(solution)/shard_map/reduce_scatter | solution.py:284
  768.5 40.7 %reduce-scatter.7.cloned.1.call-done = bf16[128,1536]{1,0:T(8,128)(2,1)} async-done(((bf16[1024,1536]{1,0:T(8,128)(2,1)}), bf16[128,1536]{1,0:T(8,128)(2,1)}) %reduce-scatter.7.cloned.1.call-update) | async-done | bytes 393232 | tf_op jit(solution)/shard_map/reduce_scatter | solution.py:299
  (277 shorter events, 104.6 us)
Async XLA Ops:
  7.2 65.9 %all-gather.7.cloned.1.call-start = ((), (), s32[]{:S(2)}) async-start(), calls=%async_computation.10 | async-start | bytes 3538944 | tf_op jit(solution)/shard_map/all_gather | solution.py:116
  7.9 113.8 %all-gather.9.cloned.1.call-start = ((), (), s32[]{:S(2)}) async-start(), calls=%async_computation.11 | async-start | bytes 5308416 | tf_op jit(solution)/shard_map/all_gather | solution.py:154
  9.6 62.8 %collective-permute-start.4 = (bf16[64,1536]{1,0:T(8,128)(2,1)}, bf16[64,1536]{1,0:T(8,128)(2,1)S(1)}, u32[]{:S(2)}, u32[]{:S(2)}) collective-permute-start(bf16[64,1536]{1,0:T(8,128)(2,1)} %slice.70), channel_id=1, source_target_pairs={{0,1},{1,3},{2,4},{3,6},{4,0},{5,5},{6,2},{7,7},{8,9},{9,11},{10,1... | collective-permute-start | bytes 589832 | tf_op jit(solution)/shard_map/ppermute | solution.py:82
  26.0 45.4 %collective-permute-start.3 = (bf16[64,1536]{1,0:T(8,128)(2,1)S(1)}, bf16[64,1536]{1,0:T(8,128)(2,1)}, u32[]{:S(2)}, u32[]{:S(2)}) collective-permute-start(bf16[64,1536]{1,0:T(8,128)(2,1)S(1)} %get-tuple-element.33), channel_id=1, source_target_pairs={{0,0},{1,2},{2,3},{3,5},{4,7},{5,4},{6,1},{7,6},{8,8},{9,10},{10,1... | collective-permute-start | bytes 589832 | tf_op jit(solution)/shard_map/ppermute | solution.py:82
  27.4 43.1 %collective-permute-start.2 = (bf16[64,1536]{1,0:T(8,128)(2,1)S(1)}, bf16[64,1536]{1,0:T(8,128)(2,1)}, u32[]{:S(2)}, u32[]{:S(2)}) collective-permute-start(bf16[64,1536]{1,0:T(8,128)(2,1)S(1)} %get-tuple-element.34), channel_id=1, source_target_pairs={{0,1},{1,2},{2,4},{3,6},{4,7},{5,3},{6,0},{7,5},{8,9},{9,10},{10,1... | collective-permute-start | bytes 589832 | tf_op jit(solution)/shard_map/ppermute | solution.py:82
  32.3 37.2 %collective-permute-start.1 = (bf16[64,1536]{1,0:T(8,128)(2,1)S(1)}, bf16[64,1536]{1,0:T(8,128)(2,1)}, u32[]{:S(2)}, u32[]{:S(2)}) collective-permute-start(bf16[64,1536]{1,0:T(8,128)(2,1)S(1)} %get-tuple-element.35), channel_id=1, source_target_pairs={{0,0},{1,1},{2,3},{3,5},{4,6},{5,2},{6,7},{7,4},{8,8},{9,9},{10,11... | collective-permute-start | bytes 589832 | tf_op jit(solution)/shard_map/ppermute | solution.py:82
  33.7 34.8 %collective-permute-start = (bf16[64,1536]{1,0:T(8,128)(2,1)S(1)}, bf16[64,1536]{1,0:T(8,128)(2,1)}, u32[]{:S(2)}, u32[]{:S(2)}) collective-permute-start(bf16[64,1536]{1,0:T(8,128)(2,1)S(1)} %get-tuple-element.36), channel_id=1, source_target_pairs={{0,0},{1,2},{2,4},{3,5},{4,7},{5,1},{6,6},{7,3},{8,8},{9,10},{10,1... | collective-permute-start | bytes 589832 | tf_op jit(solution)/shard_map/ppermute | solution.py:82
  88.5 33.3 %copy-start.2 = (bf16[128,1536]{1,0:T(8,128)(2,1)S(1)}, bf16[128,1536]{1,0:T(8,128)(2,1)}, u32[]{:S(2)}) copy-start(bf16[128,1536]{1,0:T(8,128)(2,1)} %param.24) | copy-start | bytes 1179652
  95.4 24.8 %all-to-all-start = ((bf16[8,128,192]{1,2,0:T(8,128)(2,1)}), bf16[8,128,192]{1,2,0:T(8,128)(2,1)S(1)}, u32[]{:S(2)}, u32[]{:S(2)}) async-start(bf16[8,128,192]{1,2,0:T(8,128)(2,1)} %copy.77), calls=%async_computation | async-start | bytes 786432 | tf_op jit(solution)/shard_map/all_to_all | solution.py:192
  100.1 64.3 %all-gather.11.cloned.1.call-start = ((), (), s32[]{:S(2)}) async-start(), calls=%async_computation.12 | async-start | bytes 3538944 | tf_op jit(solution)/shard_map/all_gather | solution.py:198
  127.7 75.4 %all-gather.13.cloned.1.call-start = ((), (), s32[]{:S(2)}) async-start(), calls=%async_computation.14 | async-start | bytes 3538944 | tf_op jit(solution)/shard_map/all_gather | solution.py:200
  128.3 153.4 %reduce-scatter.9.cloned.1.call-start = ((), (), s32[]{:S(2)}) async-start(), calls=%async_computation.15 | async-start | bytes 3538944 | tf_op jit(solution)/shard_map/reduce_scatter | solution.py:246
  128.6 38.9 %copy-start.22 = (bf16[24,1536]{1,0:T(8,128)(2,1)}, bf16[24,1536]{1,0:T(8,128)(2,1)S(1)}, u32[]{:S(2)}) copy-start(bf16[24,1536]{1,0:T(8,128)(2,1)S(1)} %reshape.400) | copy-start | bytes 221188
  129.2 38.1 %copy-start.30 = (s32[3,1024]{1,0:T(4,128)}, s32[3,1024]{1,0:T(4,128)S(1)}, u32[]{:S(2)}) copy-start(s32[3,1024]{1,0:T(4,128)S(1)} %fusion.41) | copy-start | bytes 36868
  164.4 14.0 %slice-start.7 = ((s8[4718592]{0:T(1024)(128)(4,1)}), s8[4194304]{0:T(1024)(128)(4,1)S(1)}, s32[]{:S(2)}) async-start(s8[4718592]{0:T(1024)(128)(4,1)} %bitcast.261), calls=%async_computation.30 | async-start | bytes 8388608
  209.2 10.9 %copy-start.7 = (bf16[1152,1536]{1,0:T(8,128)(2,1)}, bf16[1152,1536]{1,0:T(8,128)(2,1)S(1)}, u32[]{:S(2)}) copy-start(bf16[1152,1536]{1,0:T(8,128)(2,1)S(1)} %convolution_convert_fusion) | copy-start | bytes 10616836
  209.3 10.9 %copy-start.52 = (f32[3,384,512]{2,1,0:T(8,128)S(1)}, f32[3,384,512]{2,1,0:T(8,128)}, u32[]{:S(2)}) copy-start(f32[3,384,512]{2,1,0:T(8,128)} %copy-done.51) | copy-start | bytes 7077892
  209.3 10.9 %copy-start.53 = (f32[3,384,512]{2,1,0:T(8,128)S(1)}, f32[3,384,512]{2,1,0:T(8,128)}, u32[]{:S(2)}) copy-start(f32[3,384,512]{2,1,0:T(8,128)} %get-tuple-element.51) | copy-start | bytes 7077892
  209.3 17.1 %slice-start.5 = ((s8[4718592]{0:T(1024)(128)(4,1)}), s8[4194304]{0:T(1024)(128)(4,1)S(1)}, s32[]{:S(2)}) async-start(s8[4718592]{0:T(1024)(128)(4,1)} %bitcast.236), calls=%async_computation.28 | async-start | bytes 8388608
  242.0 9.6 %all-to-all-start.1 = ((f32[3,8,128]{2,0,1:T(4,128)}), f32[3,8,128]{2,0,1:T(4,128)}, u32[]{:S(2)}, u32[]{:S(2)}) async-start(f32[3,8,128]{2,0,1:T(4,128)} %bitcast.258), calls=%async_computation.3 | async-start | bytes 32768 | tf_op jit(solution)/shard_map/all_to_all | solution.py:247
  293.0 16.6 %all-to-all-start.2 = ((bf16[128,8,192]{0,2,1:T(8,128)(2,1)}), bf16[128,8,192]{0,2,1:T(8,128)(2,1)}, u32[]{:S(2)}, u32[]{:S(2)}) async-start(bf16[128,8,192]{0,2,1:T(8,128)(2,1)} %bitcast.245), calls=%async_computation.4 | async-start | bytes 786432 | tf_op jit(solution)/shard_map/all_to_all | solution.py:263
  297.1 50.8 %all-gather.15.cloned.1.call-start = ((), (), s32[]{:S(2)}) async-start(), calls=%async_computation.17 | async-start | bytes 3538944 | tf_op jit(solution)/shard_map/all_gather | solution.py:201
  309.6 38.3 %all-to-all-start.3 = ((bf16[128,8,192]{0,2,1:T(8,128)(2,1)}), bf16[128,8,192]{0,2,1:T(8,128)(2,1)}, u32[]{:S(2)}, u32[]{:S(2)}) async-start(bf16[128,8,192]{0,2,1:T(8,128)(2,1)} %bitcast.244), calls=%async_computation.6 | async-start | bytes 786432 | tf_op jit(solution)/shard_map/all_to_all | solution.py:266
  313.7 165.1 %all-reduce.4.cloned.1.call-start = ((), (), s32[]{:S(2)}) async-start(), calls=%async_computation.18 | async-start | bytes 393216 | tf_op jit(solution)/shard_map/psum | solution.py:289
  324.5 11.8 %slice-start = ((s8[12582912]{0:T(1024)(128)(4,1)}), s8[4194304]{0:T(1024)(128)(4,1)S(1)}, s32[]{:S(2)}) async-start(s8[12582912]{0:T(1024)(128)(4,1)} %bitcast.232), calls=%async_computation.23 | async-start | bytes 8388608
  324.6 11.8 %slice-start.1 = ((s8[12582912]{0:T(1024)(128)(4,1)}), s8[4194304]{0:T(1024)(128)(4,1)S(1)}, s32[]{:S(2)}) async-start(s8[12582912]{0:T(1024)(128)(4,1)} %bitcast.232), calls=%async_computation.24 | async-start | bytes 8388608
  343.4 201.4 %all-reduce.6.cloned.1.call-start = ((), (), s32[]{:S(2)}) async-start(), calls=%async_computation.22 | async-start | bytes 3145728 | tf_op jit(solution)/shard_map/psum | solution.py:294
  351.9 252.9 %reduce-scatter.17.cloned.1.call-start = ((), (), s32[]{:S(2)}) async-start(), calls=%async_computation.21 | async-start | bytes 5898240 | tf_op jit(solution)/shard_map/reduce_scatter | solution.py:225
  373.6 291.0 %reduce-scatter.15.cloned.1.call-start = ((), (), s32[]{:S(2)}) async-start(), calls=%async_computation.20 | async-start | bytes 5898240 | tf_op jit(solution)/shard_map/reduce_scatter | solution.py:225
  393.6 331.0 %reduce-scatter.13.cloned.1.call-start = ((), (), s32[]{:S(2)}) async-start(), calls=%async_computation.19 | async-start | bytes 5898240 | tf_op jit(solution)/shard_map/reduce_scatter | solution.py:225
  413.6 353.6 %reduce-scatter.11.cloned.1.call-start = ((), (), s32[]{:S(2)}) async-start(), calls=%async_computation.16 | async-start | bytes 3538944 | tf_op jit(solution)/shard_map/reduce_scatter | solution.py:284
  414.1 395.1 %reduce-scatter.7.cloned.1.call-start = ((), (), s32[]{:S(2)}) async-start(), calls=%async_computation.13 | async-start | bytes 3538944 | tf_op jit(solution)/shard_map/reduce_scatter | solution.py:299
  414.5 11.0 %copy-start.49 = (s32[8]{0:T(128)S(1)}, s32[8]{0:T(128)}, u32[]{:S(2)}) copy-start(s32[8]{0:T(128)} %constant.111.clone) | copy-start | bytes 100
  414.5 12.9 %copy-start.48 = (s32[8]{0:T(128)S(1)}, s32[8]{0:T(128)}, u32[]{:S(2)}) copy-start(s32[8]{0:T(128)} %constant.110.clone) | copy-start | bytes 100
  414.5 14.7 %copy-start.47 = (s32[8]{0:T(128)S(1)}, s32[8]{0:T(128)}, u32[]{:S(2)}) copy-start(s32[8]{0:T(128)} %constant.109.clone) | copy-start | bytes 100
  414.5 16.6 %copy-start.46 = (s32[8]{0:T(128)S(1)}, s32[8]{0:T(128)}, u32[]{:S(2)}) copy-start(s32[8]{0:T(128)} %constant.108.clone) | copy-start | bytes 100
  414.5 22.5 %copy-start.3 = (bf16[128,1536]{1,0:T(8,128)(2,1)S(1)}, bf16[128,1536]{1,0:T(8,128)(2,1)}, u32[]{:S(2)}) copy-start(bf16[128,1536]{1,0:T(8,128)(2,1)} %param.24) | copy-start | bytes 1179652
  546.2 14.6 %collective-permute-start.5 = (bf16[64,1536]{1,0:T(8,128)(2,1)S(1)}, bf16[64,1536]{1,0:T(8,128)(2,1)S(1)}, u32[]{:S(2)}, u32[]{:S(2)}) collective-permute-start(bf16[64,1536]{1,0:T(8,128)(2,1)S(1)} %get-tuple-element.32), channel_id=1, source_target_pairs={{0,0},{2,1},{4,2},{5,3},{7,4},{1,5},{6,6},{3,7},{8,8},{10,9},{12,1... | collective-permute-start | bytes 589832 | tf_op jit(solution)/shard_map/ppermute | solution.py:82
  547.5 15.1 %collective-permute-start.9 = (bf16[64,1536]{1,0:T(8,128)(2,1)S(1)}, bf16[64,1536]{1,0:T(8,128)(2,1)S(1)}, u32[]{:S(2)}, u32[]{:S(2)}) collective-permute-start(bf16[64,1536]{1,0:T(8,128)(2,1)S(1)} %get-tuple-element.28), channel_id=1, source_target_pairs={{1,0},{3,1},{4,2},{6,3},{0,4},{5,5},{2,6},{7,7},{9,8},{11,9},{12,1... | collective-permute-start | bytes 589832 | tf_op jit(solution)/shard_map/ppermute | solution.py:82
  553.6 9.0 %collective-permute-start.8 = (bf16[64,1536]{1,0:T(8,128)(2,1)S(1)}, bf16[64,1536]{1,0:T(8,128)(2,1)S(1)}, u32[]{:S(2)}, u32[]{:S(2)}) collective-permute-start(bf16[64,1536]{1,0:T(8,128)(2,1)S(1)} %get-tuple-element.29), channel_id=1, source_target_pairs={{0,0},{2,1},{3,2},{5,3},{7,4},{4,5},{1,6},{6,7},{8,8},{10,9},{11,1... | collective-permute-start | bytes 589832 | tf_op jit(solution)/shard_map/ppermute | solution.py:82
  554.3 8.3 %collective-permute-start.7 = (bf16[64,1536]{1,0:T(8,128)(2,1)S(1)}, bf16[64,1536]{1,0:T(8,128)(2,1)S(1)}, u32[]{:S(2)}, u32[]{:S(2)}) collective-permute-start(bf16[64,1536]{1,0:T(8,128)(2,1)S(1)} %get-tuple-element.30), channel_id=1, source_target_pairs={{1,0},{2,1},{4,2},{6,3},{7,4},{3,5},{0,6},{5,7},{9,8},{10,9},{12,1... | collective-permute-start | bytes 589832 | tf_op jit(solution)/shard_map/ppermute | solution.py:82
  557.9 2.9 collective-permute-start.6
  664.6 102.6 %copy-start.45 = (f32[128]{0:T(128)S(1)}, f32[128]{0:T(128)}, u32[]{:S(2)}) copy-start(f32[128]{0:T(128)} %add_rsqrt_fusion.1) | copy-start | bytes 1540
  664.6 144.6 %copy-start.1 = (f32[128,1536]{1,0:T(8,128)S(1)}, f32[128,1536]{1,0:T(8,128)}, u32[]{:S(2)}) copy-start(f32[128,1536]{1,0:T(8,128)} %copy-done) | copy-start | bytes 2359300
  664.6 144.6 %copy-start.5 = (f32[128,1536]{1,0:T(8,128)S(1)}, f32[128,1536]{1,0:T(8,128)}, u32[]{:S(2)}) copy-start(f32[128,1536]{1,0:T(8,128)} %copy-done.4) | copy-start | bytes 2359300
  664.7 144.6 %copy-start.9 = (bf16[128,1536]{1,0:T(8,128)(2,1)S(1)}, bf16[128,1536]{1,0:T(8,128)(2,1)}, u32[]{:S(2)}) copy-start(bf16[128,1536]{1,0:T(8,128)(2,1)} %param.35) | copy-start | bytes 1179652
  664.7 144.6 %copy-start.38 = (f32[128]{0:T(128)S(1)}, f32[128]{0:T(128)}, u32[]{:S(2)}) copy-start(f32[128]{0:T(128)} %copy-done.37) | copy-start | bytes 1540
  664.7 144.6 %copy-start.44 = (f32[128]{0:T(128)S(1)}, f32[128]{0:T(128)}, u32[]{:S(2)}) copy-start(f32[128]{0:T(128)} %copy-done.43) | copy-start | bytes 1540
  (43 other events, 194.6 us)
Sparse Core Ops, SparseCore 0:
  9.6 49.7 all-gather.6
  61.1 60.6 all-gather.8
  127.8 36.5 all-gather.10
  165.9 37.1 all-gather.12
  242.1 39.5 reduce-scatter.8
  299.2 48.1 all-gather.14
  353.5 125.2 all-reduce.3
  483.1 61.6 all-reduce.5
  547.8 56.9 reduce-scatter.16
  607.7 56.9 reduce-scatter.14
  667.6 56.9 reduce-scatter.12
  726.8 40.3 reduce-scatter.10
  769.5 39.6 reduce-scatter.6
where the time goes:
time: 829 us; the launch traced here: 819 us
  waiting for transfers between devices  458 us (55%)
  matrix products  134 us (16%)
  local copies, waits for them, and re-layouts  83.2 us (10%)
  other arithmetic  41.9 us (5%)
  starting transfers between devices  41.2 us (5%)
  between operations  33 us (4%)
  blocking collectives  27.3 us (3%)
    reduce_scatter x3, waiting for transfers between devices, grp_sum(): total = lax.psum_scatter(part, 'grp', scatter_dimension=0, tiled=True)  154 us
    psum x1, waiting for transfers between devices, local(): qkv_sum = lax.psum(qkv_grad.astype(bf16), 'grp')  63.6 us
    reshape x6, local copies, waits for them, and re-layouts, shares(): grad.reshape(mine * hidden, copies, width // copies).transpose(1, 0, 2)  42.6 us
    psum x1, waiting for transfers between devices, local(): lax.psum(jnp.concatenate([router_grad, gain_one_grad, gain_two_grad], axi...  41.1 us
    reduce_scatter x1, waiting for transfers between devices, local(): returned = lax.psum_scatter(out_part, 'ep', scatter_dimension=0, tiled=True)  40.7 us
    reduce_scatter x1, waiting for transfers between devices, local(): lax.psum_scatter(one_part.astype(bf16), 'ep', scatter_dimension=0, tiled=...  39.7 us
    all_gather x1, waiting for transfers between devices, local(): x_two_all = lax.all_gather(x_two, 'ep', axis=0, tiled=True)  33.4 us
    all_gather x1, blocking collectives, local(): small_all = lax.all_gather(small, 'ep', axis=0, tiled=False)  27.3 us
  transfers between devices with their start and end apart: 27, of which 15 were waited for; matrix products, arithmetic and copies ran while one was open for 24% of the time, Pallas kernels for 0%

commit v1 on v0

--- a/solution.py
+++ b/solution.py
@@ -189,7 +189,12 @@
     prob_low = prob.astype(bf16)
     attended = jnp.einsum("hgqk,hkd->hgqd", prob_low, value, preferred_element_type=f32)
     mixed_heads = attended.transpose(2, 0, 1, 3).reshape(seq, heads * hd).astype(bf16)
-    mixed = lax.all_to_all(mixed_heads, "ep", split_axis=0, concat_axis=1, tiled=True)
+    mixed = jnp.concatenate(
+        jax.lax.all_to_all(
+            jnp.stack(jnp.split(mixed_heads, jax.lax.axis_size("ep"), axis=0)), "ep", 0, 0
+        ),
+        1,
+    )
     branch = jnp.einsum("tc,dc->td", mixed, full_out, preferred_element_type=f32)
     hidden_one = layer_in.astype(f32) + branch
     scale_two = lax.rsqrt(jnp.mean(hidden_one * hidden_one, axis=-1, keepdims=True) + eps)

time: 829 us -> 828 us (level)
  transfers between devices with their start and end apart: 27 -> 27, of which waited for: 15 -> 14; matrix products, arithmetic and copies ran while one was open for 24% -> 24% of each run, Pallas kernels for 0% -> 0%
where the time goes in v1:
time: 828 us; the launch traced here: 817 us
  waiting for transfers between devices  453 us (55%)
  matrix products  134 us (16%)
  local copies, waits for them, and re-layouts  87.5 us (11%)
  other arithmetic  42 us (5%)
  starting transfers between devices  41.2 us (5%)
  between operations  33 us (4%)
  blocking collectives  27.2 us (3%)
    reduce_scatter x3, waiting for transfers between devices, grp_sum(): total = lax.psum_scatter(part, 'grp', scatter_dimension=0, tiled=True)  154 us
    psum x1, waiting for transfers between devices, local(): qkv_sum = lax.psum(qkv_grad.astype(bf16), 'grp')  63.6 us
    reshape x6, local copies, waits for them, and re-layouts, shares(): grad.reshape(mine * hidden, copies, width // copies).transpose(1, 0, 2)  42.7 us
    psum x1, waiting for transfers between devices, local(): lax.psum(jnp.concatenate([router_grad, gain_one_grad, gain_two_grad], axi...  40.9 us
    reduce_scatter x1, waiting for transfers between devices, local(): returned = lax.psum_scatter(out_part, 'ep', scatter_dimension=0, tiled=True)  40.7 us
    reduce_scatter x1, waiting for transfers between devices, local(): lax.psum_scatter(one_part.astype(bf16), 'ep', scatter_dimension=0, tiled=...  39.7 us
    all_gather x1, waiting for transfers between devices, local(): x_two_all = lax.all_gather(x_two, 'ep', axis=0, tiled=True)  33.7 us
    all_gather x1, blocking collectives, local(): small_all = lax.all_gather(small, 'ep', axis=0, tiled=False)  27.2 us
  transfers between devices with their start and end apart: 27, of which 14 were waited for; matrix products, arithmetic and copies ran while one was open for 24% of the time, Pallas kernels for 0%

profile of v1, /device:TPU:0, one launch (start us, length us, event | category | flops | bytes accessed | tf_op | source)
XLA Modules:
  0.0 817.3 jit_solution(12486724100422439647)
XLA Ops:
  27.4 5.0 collective-permute-start.2
  38.5 27.2 %all-gather = bf16[49152]{0:T(1024)(128)(2,1)S(1)} all-gather(bf16[6144]{0:T(1024)(128)(2,1)S(1)} %concatenate.21), channel_id=2, replica_groups=mesh['grp'=4,'ep'=8] {'ep'}, dimensions={0}, use_global_device_ids=true | all-gather | bytes 110592 | tf_op jit(solution)/shard_map/all_gather | solution.py:127
  76.0 3.2 fusion.48
  80.3 8.0 fusion.91
  88.4 6.1 fusion.32
  99.6 4.6 all-to-all-start
  104.4 15.8 %all-to-all-done = bf16[8,128,192]{1,2,0:T(8,128)(2,1)S(1)} async-done(((bf16[8,128,192]{1,2,0:T(8,128)(2,1)}), bf16[8,128,192]{1,2,0:T(8,128)(2,1)S(1)}, u32[]{:S(2)}, u32[]{:S(2)}) %all-to-all-start) | async-done | bytes 393248 | tf_op jit(solution)/shard_map/all_to_all | solution.py:193
  120.2 4.2 multiply_reduce_fusion.3
  129.6 33.7 %all-gather.11.cloned.1.call-done = bf16[1024,1536]{1,0:T(8,128)(2,1)} async-done(((bf16[128,1536]{1,0:T(8,128)(2,1)}), bf16[1024,1536]{1,0:T(8,128)(2,1)}) %all-gather.11.cloned.1.call-update) | async-done | bytes 3145744 | tf_op jit(solution)/shard_map/all_gather | solution.py:203
  167.6 6.2 convolution_convert_fusion.1
  177.2 3.9 multiply_convert_fusion.5
  181.1 20.8 %all-gather.13.cloned.1.call-done = bf16[1024,1536]{1,0:T(8,128)(2,1)} async-done(((bf16[128,1536]{1,0:T(8,128)(2,1)}), bf16[1024,1536]{1,0:T(8,128)(2,1)}) %all-gather.13.cloned.1.call-update) | async-done | bytes 3145744 | tf_op jit(solution)/shard_map/all_gather | solution.py:205
  201.9 6.2 convolution_convert_fusion
  208.2 9.0 %fusion.5 = (f32[3,384]{1,0:T(4,128)S(1)}, f32[3,384,1536]{2,1,0:T(8,128)}) fusion(bf16[3,384,1536]{2,1,0:T(8,128)(2,1)S(1)} %bitcast.242, bf16[3,384,512]{2,1,0:T(8,128)(2,1)S(1)} %copy-done.18, bf16[3,512,1536]{2,1,0:T(8,128)(2,1)} %param.34), kind=kOutput, calls=%fused_computation.17 | convolution fusion | flops 1817246592 | bytes 16519680 | tf_op jit(solution)/shard_map/jcf,jfd->jcd/dot_general | solution.py:239
  219.1 6.2 multiply_convert_fusion.3
  225.3 4.9 fusion.98
  230.2 10.6 %bitcast_convert_fusion = bf16[1024,1536]{1,0:T(8,128)(2,1)} fusion(s32[3,1024]{1,0:T(4,128)} %copy-done.30, f32[3,384,1536]{2,1,0:T(8,128)} %fusion.98, bf16[3,384,512]{2,1,0:T(8,128)(2,1)} %get-tuple-element.22, bf16[3,512,1536]{2,1,0:T(8,128)(2,1)} %param.33), kind=kOutput, calls=%fused_computation.23 | convolution fusion | flops 5442109440 | bytes 16134144 | tf_op jit(solution)/shard_map/pt,pd->td/dot_general | solution.py:219
  240.9 3.9 all-to-all-start.1
  244.8 5.7 all-to-all-done.1
  253.9 26.7 %reduce-scatter.9.cloned.1.call-done = bf16[128,1536]{1,0:T(8,128)(2,1)} async-done(((bf16[1024,1536]{1,0:T(8,128)(2,1)}), bf16[128,1536]{1,0:T(8,128)(2,1)}) %reduce-scatter.9.cloned.1.call-update) | async-done | bytes 393232 | tf_op jit(solution)/shard_map/reduce_scatter | solution.py:251
  286.1 3.9 convolution_convert_fusion.7
  291.9 4.1 all-to-all-start.2
  301.6 6.9 all-to-all-done.2
  308.5 4.1 all-to-all-start.3
  316.7 6.7 multiply_reduce_fusion
  323.4 8.2 %multiply_convert_fusion = bf16[3,1024,1024]{1,2,0:T(8,128)(2,1)S(1)} fusion(f32[3,1024,1024]{1,2,0:T(8,128)S(1)} %get-tuple-element.66, f32[3,1024]{1,0:T(4,128)S(1)} %get-tuple-element.65, f32[3,1024,1024]{1,2,0:T(8,128)} %get-tuple-element.55, f32[3,1024]{1,0:T(4,128)S(1)} %copy-done.36), kind=kLoop, calls=%fused_computation.3 | loop fusion | flops 12582912 | bytes 31481856 | tf_op jit(solution)/shard_map/convert_element_type | solution.py:275
  337.6 3.9 fusion.7
  342.4 4.4 convolution_convert_fusion.5
  346.8 4.0 convolution_convert_fusion.6
  351.1 7.2 convolution_convert_fusion.2
  358.3 9.1 %reshape.435 = bf16[1536,4,384]{2,1,0:T(4,128)(2,1)} reshape(bf16[3,512,1536]{2,1,0:T(8,128)(2,1)} %convolution_convert_fusion.2) | data formatting | bytes 9437184 | tf_op jit(solution)/shard_map/reshape | solution.py:226
  367.4 5.1 copy.89
  372.6 5.7 convolution_convert_fusion.3
  378.3 9.1 %reshape.431 = bf16[1536,4,384]{2,1,0:T(4,128)(2,1)} reshape(bf16[3,512,1536]{2,1,0:T(8,128)(2,1)} %convolution_convert_fusion.3) | data formatting | bytes 9437184 | tf_op jit(solution)/shard_map/reshape | solution.py:226
  387.4 5.1 copy.87
  392.6 5.7 convolution_convert_fusion.4
  398.3 9.1 %reshape.427 = bf16[1536,4,384]{2,1,0:T(4,128)(2,1)} reshape(bf16[3,512,1536]{2,1,0:T(8,128)(2,1)} %convolution_convert_fusion.4) | data formatting | bytes 9437184 | tf_op jit(solution)/shard_map/reshape | solution.py:226
  407.4 5.1 copy.85
  413.6 9.0 %bitcast_convert_fusion.1 = bf16[1024,1536]{1,0:T(8,128)(2,1)} fusion(f32[3,384,1536]{2,1,0:T(8,128)} %get-tuple-element.61, f32[3,384]{1,0:T(4,128)S(1)} %copy-done.40, s32[3,1024]{1,0:T(4,128)S(1)} %copy-done.32), kind=kOutput, calls=%fused_computation.24 | convolution fusion | flops 3630170112 | bytes 10240512 | tf_op jit(solution)/shard_map/pt,pd->td/dot_general | solution.py:219
  436.7 40.9 %all-reduce.4.cloned.1.call-done = f32[26,1536]{1,0:T(8,128)} async-done(((f32[26,1536]{1,0:T(8,128)}), f32[26,1536]{1,0:T(8,128)}) %all-reduce.4.cloned.1.call-update) | async-done | bytes 159760 | tf_op jit(solution)/shard_map/psum | solution.py:294
  480.0 63.6 %all-reduce.6.cloned.1.call-done = (bf16[5,64,1536]{2,1,0:T(8,128)(2,1)}, bf16[192,1536]{1,0:T(8,128)(2,1)}) async-done(((bf16[5,64,1536]{2,1,0:T(8,128)(2,1)}, bf16[192,1536]{1,0:T(8,128)(2,1)}), (bf16[5,64,1536]{2,1,0:T(8,128)(2,1)}, bf16[192,1536]{1,0:T(8,128)(2,1)})) %all-reduce.6.cloned.1.call-update) | async-done | bytes 1572880 | tf_op jit(solution)/shard_map/psum | solution.py:299
  546.3 6.1 collective-permute-start.9
  553.1 3.6 collective-permute-start.7
  563.6 40.0 %reduce-scatter.17.cloned.1.call-done = bf16[1536,384]{1,0:T(8,128)(2,1)} async-done(((bf16[6144,384]{1,0:T(8,128)(2,1)}), bf16[1536,384]{1,0:T(8,128)(2,1)}) %reduce-scatter.17.cloned.1.call-update) | async-done | bytes 1179664 | tf_op jit(solution)/shard_map/reduce_scatter | solution.py:230
  606.5 57.0 %reduce-scatter.15.cloned.1.call-done = bf16[1536,384]{1,0:T(8,128)(2,1)} async-done(((bf16[6144,384]{1,0:T(8,128)(2,1)}), bf16[1536,384]{1,0:T(8,128)(2,1)}) %reduce-scatter.15.cloned.1.call-update) | async-done | bytes 1179664 | tf_op jit(solution)/shard_map/reduce_scatter | solution.py:230
  666.5 57.0 %reduce-scatter.13.cloned.1.call-done = bf16[1536,384]{1,0:T(8,128)(2,1)} async-done(((bf16[6144,384]{1,0:T(8,128)(2,1)}), bf16[1536,384]{1,0:T(8,128)(2,1)}) %reduce-scatter.13.cloned.1.call-update) | async-done | bytes 1179664 | tf_op jit(solution)/shard_map/reduce_scatter | solution.py:230
  726.3 39.7 %reduce-scatter.11.cloned.1.call-done = bf16[128,1536]{1,0:T(8,128)(2,1)} async-done(((bf16[1024,1536]{1,0:T(8,128)(2,1)}), bf16[128,1536]{1,0:T(8,128)(2,1)}) %reduce-scatter.11.cloned.1.call-update) | async-done | bytes 393232 | tf_op jit(solution)/shard_map/reduce_scatter | solution.py:289
  767.3 40.7 %reduce-scatter.7.cloned.1.call-done = bf16[128,1536]{1,0:T(8,128)(2,1)} async-done(((bf16[1024,1536]{1,0:T(8,128)(2,1)}), bf16[128,1536]{1,0:T(8,128)(2,1)}) %reduce-scatter.7.cloned.1.call-update) | async-done | bytes 393232 | tf_op jit(solution)/shard_map/reduce_scatter | solution.py:304
  (284 shorter events, 107.3 us)
Async XLA Ops:
  7.2 65.9 %all-gather.7.cloned.1.call-start = ((), (), s32[]{:S(2)}) async-start(), calls=%async_computation.10 | async-start | bytes 3538944 | tf_op jit(solution)/shard_map/all_gather | solution.py:116
  7.9 112.3 %all-gather.9.cloned.1.call-start = ((), (), s32[]{:S(2)}) async-start(), calls=%async_computation.11 | async-start | bytes 5308416 | tf_op jit(solution)/shard_map/all_gather | solution.py:154
  9.6 62.8 %collective-permute-start.4 = (bf16[64,1536]{1,0:T(8,128)(2,1)}, bf16[64,1536]{1,0:T(8,128)(2,1)S(1)}, u32[]{:S(2)}, u32[]{:S(2)}) collective-permute-start(bf16[64,1536]{1,0:T(8,128)(2,1)} %slice.78), channel_id=1, source_target_pairs={{0,1},{1,3},{2,4},{3,6},{4,0},{5,5},{6,2},{7,7},{8,9},{9,11},{10,1... | collective-permute-start | bytes 589832 | tf_op jit(solution)/shard_map/ppermute | solution.py:82
  26.0 45.4 %collective-permute-start.3 = (bf16[64,1536]{1,0:T(8,128)(2,1)S(1)}, bf16[64,1536]{1,0:T(8,128)(2,1)}, u32[]{:S(2)}, u32[]{:S(2)}) collective-permute-start(bf16[64,1536]{1,0:T(8,128)(2,1)S(1)} %get-tuple-element.33), channel_id=1, source_target_pairs={{0,0},{1,2},{2,3},{3,5},{4,7},{5,4},{6,1},{7,6},{8,8},{9,10},{10,1... | collective-permute-start | bytes 589832 | tf_op jit(solution)/shard_map/ppermute | solution.py:82
  27.4 43.1 %collective-permute-start.2 = (bf16[64,1536]{1,0:T(8,128)(2,1)S(1)}, bf16[64,1536]{1,0:T(8,128)(2,1)}, u32[]{:S(2)}, u32[]{:S(2)}) collective-permute-start(bf16[64,1536]{1,0:T(8,128)(2,1)S(1)} %get-tuple-element.34), channel_id=1, source_target_pairs={{0,1},{1,2},{2,4},{3,6},{4,7},{5,3},{6,0},{7,5},{8,9},{9,10},{10,1... | collective-permute-start | bytes 589832 | tf_op jit(solution)/shard_map/ppermute | solution.py:82
  32.3 37.2 %collective-permute-start.1 = (bf16[64,1536]{1,0:T(8,128)(2,1)S(1)}, bf16[64,1536]{1,0:T(8,128)(2,1)}, u32[]{:S(2)}, u32[]{:S(2)}) collective-permute-start(bf16[64,1536]{1,0:T(8,128)(2,1)S(1)} %get-tuple-element.35), channel_id=1, source_target_pairs={{0,0},{1,1},{2,3},{3,5},{4,6},{5,2},{6,7},{7,4},{8,8},{9,9},{10,11... | collective-permute-start | bytes 589832 | tf_op jit(solution)/shard_map/ppermute | solution.py:82
  33.6 34.9 %collective-permute-start = (bf16[64,1536]{1,0:T(8,128)(2,1)S(1)}, bf16[64,1536]{1,0:T(8,128)(2,1)}, u32[]{:S(2)}, u32[]{:S(2)}) collective-permute-start(bf16[64,1536]{1,0:T(8,128)(2,1)S(1)} %get-tuple-element.36), channel_id=1, source_target_pairs={{0,0},{1,2},{2,4},{3,5},{4,7},{5,1},{6,6},{7,3},{8,8},{9,10},{10,1... | collective-permute-start | bytes 589832 | tf_op jit(solution)/shard_map/ppermute | solution.py:82
  88.4 31.8 %copy-start.2 = (bf16[128,1536]{1,0:T(8,128)(2,1)S(1)}, bf16[128,1536]{1,0:T(8,128)(2,1)}, u32[]{:S(2)}) copy-start(bf16[128,1536]{1,0:T(8,128)(2,1)} %param.24) | copy-start | bytes 1179652
  99.6 20.6 %all-to-all-start = ((bf16[8,128,192]{1,2,0:T(8,128)(2,1)}), bf16[8,128,192]{1,2,0:T(8,128)(2,1)S(1)}, u32[]{:S(2)}, u32[]{:S(2)}) async-start(bf16[8,128,192]{1,2,0:T(8,128)(2,1)} %constant_dynamic-update-slice_fusion), calls=%async_computation | async-start | bytes 786432 | tf_op jit(solution)/shard_map/all_to_all | solution.py:193
  104.2 59.0 %all-gather.11.cloned.1.call-start = ((), (), s32[]{:S(2)}) async-start(), calls=%async_computation.12 | async-start | bytes 3538944 | tf_op jit(solution)/shard_map/all_gather | solution.py:203
  126.3 75.7 %all-gather.13.cloned.1.call-start = ((), (), s32[]{:S(2)}) async-start(), calls=%async_computation.14 | async-start | bytes 3538944 | tf_op jit(solution)/shard_map/all_gather | solution.py:205
  126.8 153.7 %reduce-scatter.9.cloned.1.call-start = ((), (), s32[]{:S(2)}) async-start(), calls=%async_computation.15 | async-start | bytes 3538944 | tf_op jit(solution)/shard_map/reduce_scatter | solution.py:251
  127.2 39.2 %copy-start.22 = (bf16[24,1536]{1,0:T(8,128)(2,1)}, bf16[24,1536]{1,0:T(8,128)(2,1)S(1)}, u32[]{:S(2)}) copy-start(bf16[24,1536]{1,0:T(8,128)(2,1)S(1)} %reshape.420) | copy-start | bytes 221188
  127.8 38.4 %copy-start.30 = (s32[3,1024]{1,0:T(4,128)}, s32[3,1024]{1,0:T(4,128)S(1)}, u32[]{:S(2)}) copy-start(s32[3,1024]{1,0:T(4,128)S(1)} %fusion.44) | copy-start | bytes 36868
  163.3 14.0 %slice-start.7 = ((s8[4718592]{0:T(1024)(128)(4,1)}), s8[4194304]{0:T(1024)(128)(4,1)S(1)}, s32[]{:S(2)}) async-start(s8[4718592]{0:T(1024)(128)(4,1)} %bitcast.270), calls=%async_computation.30 | async-start | bytes 8388608
  208.1 10.9 %copy-start.7 = (bf16[1152,1536]{1,0:T(8,128)(2,1)}, bf16[1152,1536]{1,0:T(8,128)(2,1)S(1)}, u32[]{:S(2)}) copy-start(bf16[1152,1536]{1,0:T(8,128)(2,1)S(1)} %convolution_convert_fusion) | copy-start | bytes 10616836
  208.1 10.9 %copy-start.52 = (f32[3,384,512]{2,1,0:T(8,128)S(1)}, f32[3,384,512]{2,1,0:T(8,128)}, u32[]{:S(2)}) copy-start(f32[3,384,512]{2,1,0:T(8,128)} %copy-done.51) | copy-start | bytes 7077892
  208.1 10.9 %copy-start.53 = (f32[3,384,512]{2,1,0:T(8,128)S(1)}, f32[3,384,512]{2,1,0:T(8,128)}, u32[]{:S(2)}) copy-start(f32[3,384,512]{2,1,0:T(8,128)} %get-tuple-element.59) | copy-start | bytes 7077892
  208.2 17.1 %slice-start.5 = ((s8[4718592]{0:T(1024)(128)(4,1)}), s8[4194304]{0:T(1024)(128)(4,1)S(1)}, s32[]{:S(2)}) async-start(s8[4718592]{0:T(1024)(128)(4,1)} %bitcast.239), calls=%async_computation.28 | async-start | bytes 8388608
  240.9 9.6 %all-to-all-start.1 = ((f32[3,8,128]{2,0,1:T(4,128)}), f32[3,8,128]{2,0,1:T(4,128)}, u32[]{:S(2)}, u32[]{:S(2)}) async-start(f32[3,8,128]{2,0,1:T(4,128)} %bitcast.267), calls=%async_computation.3 | async-start | bytes 32768 | tf_op jit(solution)/shard_map/all_to_all | solution.py:252
  291.9 16.6 %all-to-all-start.2 = ((bf16[128,8,192]{0,2,1:T(8,128)(2,1)}), bf16[128,8,192]{0,2,1:T(8,128)(2,1)}, u32[]{:S(2)}, u32[]{:S(2)}) async-start(bf16[128,8,192]{0,2,1:T(8,128)(2,1)} %bitcast.248), calls=%async_computation.4 | async-start | bytes 786432 | tf_op jit(solution)/shard_map/all_to_all | solution.py:268
  296.0 50.8 %all-gather.15.cloned.1.call-start = ((), (), s32[]{:S(2)}) async-start(), calls=%async_computation.17 | async-start | bytes 3538944 | tf_op jit(solution)/shard_map/all_gather | solution.py:206
  308.5 38.3 %all-to-all-start.3 = ((bf16[128,8,192]{0,2,1:T(8,128)(2,1)}), bf16[128,8,192]{0,2,1:T(8,128)(2,1)}, u32[]{:S(2)}, u32[]{:S(2)}) async-start(bf16[128,8,192]{0,2,1:T(8,128)(2,1)} %bitcast.247), calls=%async_computation.6 | async-start | bytes 786432 | tf_op jit(solution)/shard_map/all_to_all | solution.py:271
  312.6 165.1 %all-reduce.4.cloned.1.call-start = ((), (), s32[]{:S(2)}) async-start(), calls=%async_computation.18 | async-start | bytes 393216 | tf_op jit(solution)/shard_map/psum | solution.py:294
  323.4 11.8 %slice-start = ((s8[12582912]{0:T(1024)(128)(4,1)}), s8[4194304]{0:T(1024)(128)(4,1)S(1)}, s32[]{:S(2)}) async-start(s8[12582912]{0:T(1024)(128)(4,1)} %bitcast.235), calls=%async_computation.23 | async-start | bytes 8388608
  323.4 11.8 %slice-start.1 = ((s8[12582912]{0:T(1024)(128)(4,1)}), s8[4194304]{0:T(1024)(128)(4,1)S(1)}, s32[]{:S(2)}) async-start(s8[12582912]{0:T(1024)(128)(4,1)} %bitcast.235), calls=%async_computation.24 | async-start | bytes 8388608
  342.3 201.3 %all-reduce.6.cloned.1.call-start = ((), (), s32[]{:S(2)}) async-start(), calls=%async_computation.22 | async-start | bytes 3145728 | tf_op jit(solution)/shard_map/psum | solution.py:299
  350.8 252.8 %reduce-scatter.17.cloned.1.call-start = ((), (), s32[]{:S(2)}) async-start(), calls=%async_computation.21 | async-start | bytes 5898240 | tf_op jit(solution)/shard_map/reduce_scatter | solution.py:230
  372.5 291.0 %reduce-scatter.15.cloned.1.call-start = ((), (), s32[]{:S(2)}) async-start(), calls=%async_computation.20 | async-start | bytes 5898240 | tf_op jit(solution)/shard_map/reduce_scatter | solution.py:230
  392.6 330.9 %reduce-scatter.13.cloned.1.call-start = ((), (), s32[]{:S(2)}) async-start(), calls=%async_computation.19 | async-start | bytes 5898240 | tf_op jit(solution)/shard_map/reduce_scatter | solution.py:230
  412.6 353.4 %reduce-scatter.11.cloned.1.call-start = ((), (), s32[]{:S(2)}) async-start(), calls=%async_computation.16 | async-start | bytes 3538944 | tf_op jit(solution)/shard_map/reduce_scatter | solution.py:289
  413.2 394.8 %reduce-scatter.7.cloned.1.call-start = ((), (), s32[]{:S(2)}) async-start(), calls=%async_computation.13 | async-start | bytes 3538944 | tf_op jit(solution)/shard_map/reduce_scatter | solution.py:304
  413.5 11.0 %copy-start.49 = (s32[8]{0:T(128)S(1)}, s32[8]{0:T(128)}, u32[]{:S(2)}) copy-start(s32[8]{0:T(128)} %constant.111.clone) | copy-start | bytes 100
  413.5 12.9 %copy-start.48 = (s32[8]{0:T(128)S(1)}, s32[8]{0:T(128)}, u32[]{:S(2)}) copy-start(s32[8]{0:T(128)} %constant.110.clone) | copy-start | bytes 100
  413.5 14.7 %copy-start.47 = (s32[8]{0:T(128)S(1)}, s32[8]{0:T(128)}, u32[]{:S(2)}) copy-start(s32[8]{0:T(128)} %constant.109.clone) | copy-start | bytes 100
  413.5 16.6 %copy-start.46 = (s32[8]{0:T(128)S(1)}, s32[8]{0:T(128)}, u32[]{:S(2)}) copy-start(s32[8]{0:T(128)} %constant.108.clone) | copy-start | bytes 100
  413.6 22.5 %copy-start.3 = (bf16[128,1536]{1,0:T(8,128)(2,1)S(1)}, bf16[128,1536]{1,0:T(8,128)(2,1)}, u32[]{:S(2)}) copy-start(bf16[128,1536]{1,0:T(8,128)(2,1)} %param.24) | copy-start | bytes 1179652
  545.0 14.6 %collective-permute-start.5 = (bf16[64,1536]{1,0:T(8,128)(2,1)S(1)}, bf16[64,1536]{1,0:T(8,128)(2,1)S(1)}, u32[]{:S(2)}, u32[]{:S(2)}) collective-permute-start(bf16[64,1536]{1,0:T(8,128)(2,1)S(1)} %get-tuple-element.32), channel_id=1, source_target_pairs={{0,0},{2,1},{4,2},{5,3},{7,4},{1,5},{6,6},{3,7},{8,8},{10,9},{12,1... | collective-permute-start | bytes 589832 | tf_op jit(solution)/shard_map/ppermute | solution.py:82
  546.3 15.1 %collective-permute-start.9 = (bf16[64,1536]{1,0:T(8,128)(2,1)S(1)}, bf16[64,1536]{1,0:T(8,128)(2,1)S(1)}, u32[]{:S(2)}, u32[]{:S(2)}) collective-permute-start(bf16[64,1536]{1,0:T(8,128)(2,1)S(1)} %get-tuple-element.28), channel_id=1, source_target_pairs={{1,0},{3,1},{4,2},{6,3},{0,4},{5,5},{2,6},{7,7},{9,8},{11,9},{12,1... | collective-permute-start | bytes 589832 | tf_op jit(solution)/shard_map/ppermute | solution.py:82
  552.4 9.0 %collective-permute-start.8 = (bf16[64,1536]{1,0:T(8,128)(2,1)S(1)}, bf16[64,1536]{1,0:T(8,128)(2,1)S(1)}, u32[]{:S(2)}, u32[]{:S(2)}) collective-permute-start(bf16[64,1536]{1,0:T(8,128)(2,1)S(1)} %get-tuple-element.29), channel_id=1, source_target_pairs={{0,0},{2,1},{3,2},{5,3},{7,4},{4,5},{1,6},{6,7},{8,8},{10,9},{11,1... | collective-permute-start | bytes 589832 | tf_op jit(solution)/shard_map/ppermute | solution.py:82
  553.1 8.3 %collective-permute-start.7 = (bf16[64,1536]{1,0:T(8,128)(2,1)S(1)}, bf16[64,1536]{1,0:T(8,128)(2,1)S(1)}, u32[]{:S(2)}, u32[]{:S(2)}) collective-permute-start(bf16[64,1536]{1,0:T(8,128)(2,1)S(1)} %get-tuple-element.30), channel_id=1, source_target_pairs={{1,0},{2,1},{4,2},{6,3},{7,4},{3,5},{0,6},{5,7},{9,8},{10,9},{12,1... | collective-permute-start | bytes 589832 | tf_op jit(solution)/shard_map/ppermute | solution.py:82
  556.7 2.9 collective-permute-start.6
  663.5 102.6 %copy-start.45 = (f32[128]{0:T(128)S(1)}, f32[128]{0:T(128)}, u32[]{:S(2)}) copy-start(f32[128]{0:T(128)} %add_rsqrt_fusion.1) | copy-start | bytes 1540
  663.5 144.5 %copy-start.1 = (f32[128,1536]{1,0:T(8,128)S(1)}, f32[128,1536]{1,0:T(8,128)}, u32[]{:S(2)}) copy-start(f32[128,1536]{1,0:T(8,128)} %copy-done) | copy-start | bytes 2359300
  663.5 144.5 %copy-start.5 = (f32[128,1536]{1,0:T(8,128)S(1)}, f32[128,1536]{1,0:T(8,128)}, u32[]{:S(2)}) copy-start(f32[128,1536]{1,0:T(8,128)} %copy-done.4) | copy-start | bytes 2359300
  663.5 144.5 %copy-start.9 = (bf16[128,1536]{1,0:T(8,128)(2,1)S(1)}, bf16[128,1536]{1,0:T(8,128)(2,1)}, u32[]{:S(2)}) copy-start(bf16[128,1536]{1,0:T(8,128)(2,1)} %param.35) | copy-start | bytes 1179652
  663.5 144.5 %copy-start.38 = (f32[128]{0:T(128)S(1)}, f32[128]{0:T(128)}, u32[]{:S(2)}) copy-start(f32[128]{0:T(128)} %copy-done.37) | copy-start | bytes 1540
  663.5 144.5 %copy-start.44 = (f32[128]{0:T(128)S(1)}, f32[128]{0:T(128)}, u32[]{:S(2)}) copy-start(f32[128]{0:T(128)} %copy-done.43) | copy-start | bytes 1540
  (43 other events, 193.2 us)
Sparse Core Ops, SparseCore 0:
  9.6 49.7 all-gather.6
  61.1 55.6 all-gather.8
  126.4 36.8 all-gather.10
  164.8 37.1 all-gather.12
  241.0 39.5 reduce-scatter.8
  298.0 48.1 all-gather.14
  352.4 125.2 all-reduce.3
  481.9 61.6 all-reduce.5
  546.7 56.9 reduce-scatter.16
  606.5 56.9 reduce-scatter.14
  666.5 56.9 reduce-scatter.12
  725.6 40.3 reduce-scatter.10
  768.3 39.6 reduce-scatter.6
